TPU v7x, 128 devices: a whole 4x4x4 slice. The times are simulated.
128 devices in a mesh: rep: 16 (over y, z), grp: 8 (over x, core).
Axes of the slice: x: 4, y: 4, z: 4, core: 2. Of those that a mesh axis runs over, the one named last changes fastest.
Arguments:
- grad_query: float32 [16, 2048, 2048], P('rep', 'grp'), may hold values from -100 to 100, as said below
- error_query: float32 [16, 2048, 2048], P('rep', 'grp'), may hold values from -3 to 3
- basis_query: float32 [2048, 32], replicated, may hold values from -0.125 to 0.125
- momentum_query: float32 [2048, 2048], P('grp'), may hold values from -0.6 to 0.6
- master_query: float32 [2048, 2048], P('grp'), may hold values from -6 to 6
- grad_gate: float32 [16, 2048, 256], P('rep', 'grp'), may hold values from -100 to 100, as said below
- error_gate: float32 [16, 2048, 256], P('rep', 'grp'), may hold values from -3 to 3
- basis_gate: float32 [256, 32], replicated, may hold values from -0.375 to 0.375
- momentum_gate: float32 [2048, 256], P('grp'), may hold values from -0.6 to 0.6
- master_gate: float32 [2048, 256], P('grp'), may hold values from -6 to 6
- vector_grad: float32 [16, 12800], P('rep', 'grp'), may hold values from -6 to 6
- vector_momentum: float32 [12800], P('grp'), may hold values from -0.6 to 0.6
- vector_master: float32 [12800], P('grp'), may hold values from 0.5 to 1.5
Outputs:
- new_error_query: float32 [16, 2048, 2048], P('rep', 'grp')
- new_momentum_query: float32 [2048, 2048], P('grp')
- new_master_query: float32 [2048, 2048], P('grp')
- weight_query: bfloat16 [2048, 2048], replicated
- new_basis_query: float32 [2048, 32], replicated
- new_error_gate: float32 [16, 2048, 256], P('rep', 'grp')
- new_momentum_gate: float32 [2048, 256], P('grp')
- new_master_gate: float32 [2048, 256], P('grp')
- weight_gate: bfloat16 [2048, 256], replicated
- new_basis_gate: float32 [256, 32], replicated
- new_vector_momentum: float32 [12800], P('grp')
- new_vector_master: float32 [12800], P('grp')
- weight_vector: bfloat16 [12800], replicated
Inputs may be any that keep to these rules, and one draw needn't show every extreme that they name: `grad_query`: each replica's gradient is a common part plus a replica's own part. `grad_gate`: each replica's gradient is a common part plus a replica's own part.
All inputs are finite; a program needn't handle non-finite values.
Results may differ from a plain program's by a relative error of at most 0.0006.
Values may be sent and summed in bfloat16 or wider, within the bound.
A program may use at most 128 MiB of HBM per device.

v0:
```python
import jax
import jax.numpy as jnp
from jax import lax
from jax.sharding import PartitionSpec as P

NS_STEPS = 4
highest = lax.Precision.HIGHEST


def inverse_root(gram_matrix):
    trace_value = jnp.trace(gram_matrix)
    identity = jnp.eye(gram_matrix.shape[0], dtype=jnp.float32)
    root_part = gram_matrix / trace_value
    inverse_part = identity
    for iteration in range(NS_STEPS):
        middle = 0.5 * (3.0 * identity - jnp.dot(inverse_part, root_part, precision=highest))
        root_part = jnp.dot(root_part, middle, precision=highest)
        inverse_part = jnp.dot(middle, inverse_part, precision=highest)
    return inverse_part / jnp.sqrt(trace_value)


def right_terms(merged, ortho):
    return jnp.einsum("dn,dr->nr", merged, ortho, precision=highest)


def finish(merged, ortho, new_basis, momentum, master, replicas):
    approx = jnp.dot(ortho, new_basis.T, precision=highest) / replicas
    new_error = (merged - approx)[None]
    new_momentum = 0.9 * momentum + approx
    new_master = master - 0.5 * new_momentum
    return (new_error, new_momentum, new_master)


def per_device(
    grad_query,
    error_query,
    basis_query,
    momentum_query,
    master_query,
    grad_gate,
    error_gate,
    basis_gate,
    momentum_gate,
    master_gate,
    vector_grad,
    vector_momentum,
    vector_master,
):
    replicas = lax.axis_size("rep")
    merged_query = (grad_query + error_query)[0]
    merged_gate = (grad_gate + error_gate)[0]
    local_query = jnp.dot(merged_query, basis_query, precision=highest)
    local_gate = jnp.dot(merged_gate, basis_gate, precision=highest)
    vector_local = vector_grad[0]
    vector_total = lax.psum(vector_local, "rep")
    left_query, left_gate = lax.psum((local_query, local_gate), "rep")
    gram_query, gram_gate = lax.psum(
        (
            jnp.dot(left_query.T, left_query, precision=highest),
            jnp.dot(left_gate.T, left_gate, precision=highest),
        ),
        "grp",
    )
    ortho_query = jnp.dot(left_query, inverse_root(gram_query), precision=highest)
    ortho_gate = jnp.dot(left_gate, inverse_root(gram_gate), precision=highest)
    terms_query = right_terms(merged_query, ortho_query)
    terms_gate = right_terms(merged_gate, ortho_gate)
    basis_new_query, basis_new_gate = lax.psum((terms_query, terms_gate), ("rep", "grp"))
    error_out_query, momentum_out_query, master_out_query = finish(
        merged_query, ortho_query, basis_new_query, momentum_query, master_query, replicas
    )
    error_out_gate, momentum_out_gate, master_out_gate = finish(
        merged_gate, ortho_gate, basis_new_gate, momentum_gate, master_gate, replicas
    )
    vector_mean = vector_total / replicas
    momentum_out_vector = 0.9 * vector_momentum + vector_mean
    master_out_vector = vector_master - 0.5 * momentum_out_vector
    whole_query, whole_gate, whole_vector = (
        lax.all_gather(master_out_query.astype(jnp.bfloat16), "grp", axis=0, tiled=True),
        lax.all_gather(master_out_gate.astype(jnp.bfloat16), "grp", axis=0, tiled=True),
        lax.all_gather(master_out_vector.astype(jnp.bfloat16), "grp", axis=0, tiled=True),
    )
    return (
        error_out_query,
        momentum_out_query,
        master_out_query,
        whole_query,
        basis_new_query,
        error_out_gate,
        momentum_out_gate,
        master_out_gate,
        whole_gate,
        basis_new_gate,
        momentum_out_vector,
        master_out_vector,
        whole_vector,
    )


def solution(mesh):
    in_specs = (
        P("rep", "grp", None),
        P("rep", "grp", None),
        P(),
        P("grp", None),
        P("grp", None),
        P("rep", "grp", None),
        P("rep", "grp", None),
        P(),
        P("grp", None),
        P("grp", None),
        P("rep", "grp"),
        P("grp"),
        P("grp"),
    )
    out_specs = (
        P("rep", "grp", None),
        P("grp", None),
        P("grp", None),
        P(),
        P(),
        P("rep", "grp", None),
        P("grp", None),
        P("grp", None),
        P(),
        P(),
        P("grp"),
        P("grp"),
        P(),
    )
    return jax.shard_map(
        per_device, mesh=mesh, in_specs=in_specs, out_specs=out_specs, check_vma=False
    )
```

profile of v0, /device:TPU:1, one launch (start us, length us, event | category | flops | bytes accessed | tf_op | source)
XLA Modules:
  0.0 369.3 jit_solution(9648238144526546208)
XLA Ops:
  7.2 1.3 reduce
  8.6 4.9 %fusion.2 = f32[256,32]{0,1:T(8,128)} fusion(f32[2048,32]{0,1:T(8,128)S(1)} %copy-done, f32[1,256,2048]{2,1,0:T(8,128)} %param.13, f32[1,256,2048]{2,1,0:T(8,128)} %param.14), kind=kOutput, calls=%fused_computation.4 | convolution fusion | flops 201850880 | bytes 4489216 | tf_op jit(solution)/shard_map/dot_general | solution.py:52
  13.5 1.0 fusion.15
  14.5 83.3 %all-reduce.8.cloned.1.call-done = (f32[256,32]{0,1:T(8,128)}, f32[256,32]{0,1:T(8,128)}, f32[1600]{0:T(1024)}) async-done(((f32[256,32]{0,1:T(8,128)}, f32[256,32]{0,1:T(8,128)}, f32[1600]{0:T(1024)}), (f32[256,32]{0,1:T(8,128)}, f32[256,32]{0,1:T(8,128)}, f32[1600]{0:T(1024)})) %all-reduce.8.cloned.1.call-update) | async-done | bytes 71952 | tf_op jit(solution)/shard_map/psum | solution.py:56
  97.8 1.0 fusion.29
  98.8 1.0 fusion.35
  99.8 22.7 %all-reduce.2 = (f32[32,32]{1,0:T(8,128)S(1)}, f32[32,32]{1,0:T(8,128)S(1)}) all-reduce(f32[32,32]{1,0:T(8,128)S(1)} %fusion.29, f32[32,32]{1,0:T(8,128)S(1)} %fusion.35), channel_id=1, replica_groups=mesh['rep'=16,'grp'=8] {'grp'}, use_global_device_ids=true, to_apply=%region_1.0 | all-reduce | flops 2048 | bytes 16384 | tf_op jit(solution)/shard_map/psum | solution.py:57
  122.5 0.6 select_reduce_fusion
  123.1 0.8 fusion.12
  124.0 0.8 fusion.20
  124.8 0.2 fusion.11
  125.3 0.2 fusion.10
  126.5 0.8 fusion.8
  127.4 0.8 fusion.21
  128.2 0.2 fusion.7
  128.6 0.2 fusion.6
  130.1 1.0 fusion.34
  131.1 3.8 %fusion = f32[2048,32]{0,1:T(8,128)} fusion(f32[256,32]{0,1:T(8,128)S(1)} %fusion.34, f32[1,256,2048]{2,1,0:T(8,128)S(1)} %copy-done.1, f32[1,256,2048]{2,1,0:T(8,128)} %param.14), kind=kOutput, calls=%fused_computation.2 | convolution fusion | flops 201850880 | bytes 4489216 | tf_op jit(solution)/shard_map/dn,dr->nr/dot_general | solution.py:23
  135.3 0.2 fusion.40
  135.5 0.3 fusion.13
  135.8 65.4 %psum.54 = f32[256,32]{0,1:T(8,128)S(1)} all-reduce(f32[256,32]{0,1:T(8,128)S(1)} %fusion.13), channel_id=1, replica_groups=mesh['rep'=16,'grp'=8] {'rep','grp'}, use_global_device_ids=true, to_apply=%region_7.8 | all-reduce | flops 8192 | bytes 65536 | tf_op jit(solution)/shard_map/psum | solution.py:68
  201.2 1.5 fusion.27
  202.8 74.1 %all-reduce.6.cloned.1.call-done = f32[2048,32]{0,1:T(8,128)} async-done(((f32[2048,32]{0,1:T(8,128)}), f32[2048,32]{0,1:T(8,128)}) %all-reduce.6.cloned.1.call-update) | async-done | bytes 262160 | tf_op jit(solution)/shard_map/psum | solution.py:68
  276.8 8.2 %fusion.28 = (bf16[256,2048]{1,0:T(8,128)(2,1)}, f32[256,2048]{1,0:T(8,128)}, f32[256,2048]{1,0:T(8,128)}, f32[1,256,2048]{2,1,0:T(8,128)}) fusion(f32[256,2048]{1,0:T(8,128)} %param.17, f32[256,2048]{1,0:T(8,128)} %param.16, f32[1,256,2048]{2,1,0:T(8,128)S(1)} %copy-done.1, f32[1,256,2048]{2,1,0:T(8,128)} %param.14, f32[256,32]{0,1:T(8,128)S(1)} %fusion.34, ...), kind=kOutput, calls=%fused_computation.53 | convolution fusion | flops 205520896 | bytes 16023552 | tf_op jit(solution)/shard_map/dot_general | solution.py:27
  285.1 0.6 dynamic-slice
  286.4 0.6 fusion.26
  287.0 0.2 dynamic-update-slice
  287.3 22.5 %all-reduce = bf16[12800]{0:T(1024)(128)(2,1)} all-reduce(bf16[12800]{0:T(1024)(128)(2,1)S(1)} %dynamic-update-slice), channel_id=1, replica_groups=mesh['rep'=16,'grp'=8] {'grp'}, use_global_device_ids=true, to_apply=%add | all-reduce | flops 12800 | bytes 51200
  309.7 42.8 %all-gather.3.cloned.1.call-done = bf16[2048,2048]{1,0:T(8,128)(2,1)} async-done(((bf16[256,2048]{1,0:T(8,128)(2,1)}), bf16[2048,2048]{1,0:T(8,128)(2,1)}) %all-gather.3.cloned.1.call-update) | async-done | bytes 8388624 | tf_op jit(solution)/shard_map/all_gather | solution.py:79
  352.5 8.5 %copy.33 = bf16[2048,2048]{1,0:T(8,128)(2,1)} copy(bf16[2048,2048]{1,0:T(8,128)(2,1)} %all-gather.3.cloned.1.call-done) | data formatting | bytes 16777216
  361.1 0.7 copy.34
  361.8 1.0 copy.35
  (54 shorter events, 2.3 us)
Async XLA Ops:
  7.2 1.4 copy-start
  7.2 90.6 %all-reduce.8.cloned.1.call-start = ((), (), s32[]{:S(2)}) async-start(), calls=%async_computation.3 | async-start | bytes 147456 | tf_op jit(solution)/shard_map/psum | solution.py:56
  8.6 4.9 %copy-start.2 = (f32[1,256,256]{2,1,0:T(8,128)S(1)}, f32[1,256,256]{2,1,0:T(8,128)}, u32[]{:S(2)}) copy-start(f32[1,256,256]{2,1,0:T(8,128)} %param.18) | copy-start | bytes 786436
  8.6 4.9 %copy-start.3 = (f32[1,256,256]{2,1,0:T(8,128)S(1)}, f32[1,256,256]{2,1,0:T(8,128)}, u32[]{:S(2)}) copy-start(f32[1,256,256]{2,1,0:T(8,128)} %param.19) | copy-start | bytes 786436
  8.6 4.9 %copy-start.10 = (f32[256,32]{0,1:T(8,128)S(1)}, f32[256,32]{0,1:T(8,128)}, u32[]{:S(2)}) copy-start(f32[256,32]{0,1:T(8,128)} %param.20) | copy-start | bytes 98308
  8.6 122.5 %copy-start.1 = (f32[1,256,2048]{2,1,0:T(8,128)S(1)}, f32[1,256,2048]{2,1,0:T(8,128)}, u32[]{:S(2)}) copy-start(f32[1,256,2048]{2,1,0:T(8,128)} %param.13) | copy-start | bytes 6291460
  14.5 262.4 %all-reduce.6.cloned.1.call-start = ((), (), s32[]{:S(2)}) async-start(), calls=%async_computation | async-start | bytes 524288 | tf_op jit(solution)/shard_map/psum | solution.py:68
  131.1 4.2 %copy-start.6 = (f32[256,32]{0,1:T(8,128)S(1)}, f32[256,32]{0,1:T(8,128)}, u32[]{:S(2)}) copy-start(f32[256,32]{0,1:T(8,128)} %get-tuple-element.14) | copy-start | bytes 98308
  131.1 70.1 %copy-start.7 = (f32[256,256]{1,0:T(8,128)S(1)}, f32[256,256]{1,0:T(8,128)}, u32[]{:S(2)}) copy-start(f32[256,256]{1,0:T(8,128)} %param.22) | copy-start | bytes 786436
  131.1 70.1 %copy-start.8 = (f32[256,256]{1,0:T(8,128)S(1)}, f32[256,256]{1,0:T(8,128)}, u32[]{:S(2)}) copy-start(f32[256,256]{1,0:T(8,128)} %param.21) | copy-start | bytes 786436
  134.9 174.8 %all-gather.5.cloned.1.call-start = ((), (), s32[]{:S(2)}) async-start(), calls=%async_computation.2 | async-start | bytes 1179648 | tf_op jit(solution)/shard_map/all_gather | solution.py:80
  201.2 83.9 %copy-start.9 = (f32[256,32]{0,1:T(8,128)}, f32[256,32]{0,1:T(8,128)S(1)}, u32[]{:S(2)}) copy-start(f32[256,32]{0,1:T(8,128)S(1)} %psum.54) | copy-start | bytes 98308
  202.7 82.5 %copy-start.14 = (u32[128]{0:T(128)S(1)}, u32[128]{0:T(128)}, u32[]{:S(2)}) copy-start(u32[128]{0:T(128)} %constant.33) | copy-start | bytes 1540
  202.7 83.7 %copy-start.11 = (f32[1600]{0:T(1024)S(1)}, f32[1600]{0:T(1024)}, u32[]{:S(2)}) copy-start(f32[1600]{0:T(1024)} %param.25) | copy-start | bytes 19204
  202.7 83.7 %copy-start.12 = (f32[1600]{0:T(1024)S(1)}, f32[1600]{0:T(1024)}, u32[]{:S(2)}) copy-start(f32[1600]{0:T(1024)} %param.24) | copy-start | bytes 19204
  202.7 83.7 %copy-start.13 = (f32[1600]{0:T(1024)S(1)}, f32[1600]{0:T(1024)}, u32[]{:S(2)}) copy-start(f32[1600]{0:T(1024)} %get-tuple-element.15) | copy-start | bytes 19204
  202.7 149.8 %all-gather.3.cloned.1.call-start = ((), (), s32[]{:S(2)}) async-start(), calls=%async_computation.1 | async-start | bytes 9437184 | tf_op jit(solution)/shard_map/all_gather | solution.py:79
  352.5 8.6 %copy-start.4 = (f32[2048,32]{0,1:T(8,128)S(1)}, f32[2048,32]{0,1:T(8,128)}, u32[]{:S(2)}) copy-start(f32[2048,32]{0,1:T(8,128)} %all-reduce.6.cloned.1.call-done) | copy-start | bytes 786436
  352.5 9.3 %copy-start.5 = (bf16[2048,256]{1,0:T(8,128)(2,1)S(1)}, bf16[2048,256]{1,0:T(8,128)(2,1)}, u32[]{:S(2)}) copy-start(bf16[2048,256]{1,0:T(8,128)(2,1)} %all-gather.5.cloned.1.call-done) | copy-start | bytes 3145732
Sparse Core Ops, SparseCore 0:
  14.6 83.1 all-reduce.7
  135.0 141.7 all-reduce.5
  279.3 21.1 all-gather.4
  302.7 49.7 all-gather.2
where the time goes:
time: 370 us; the launch traced here: 369 us
  waiting for transfers between devices  200 us (54%)
  blocking collectives  111 us (30%)
  matrix products  28.5 us (8%)
  between operations  16.1 us (4%)
  local copies, waits for them, and re-layouts  11.1 us (3%)
    psum x1, waiting for transfers between devices, per_device(): left_query, left_gate = lax.psum((local_query, local_gate), 'rep')  83.3 us
    psum x1, waiting for transfers between devices, per_device(): lax.psum((terms_query, terms_gate), ('rep', 'grp'))  74.1 us
    psum x1, blocking collectives, per_device(): lax.psum((terms_query, terms_gate), ('rep', 'grp'))  65.4 us
    all_gather x1, waiting for transfers between devices, per_device(): lax.all_gather(master_out_query.astype(jnp.bfloat16), 'grp', axis=0, tile...  42.8 us
    psum x1, blocking collectives, per_device(): lax.psum((jnp.dot(left_query.T, left_query, precision=highest), jnp.dot(l...  22.7 us
    unnamed x1, blocking collectives  22.5 us
    unnamed x36, local copies, waits for them, and re-layouts  11.1 us
    dot_general x2, matrix products, finish(): approx = jnp.dot(ortho, new_basis.T, precision=highest) / replicas  9.7 us
  transfers between devices with their start and end apart: 4, of which 3 were waited for; matrix products, arithmetic and copies ran while one was open for 3% of the time, Pallas kernels for 0%

commit v1 on v0

--- a/solution.py
+++ b/solution.py
@@ -5,6 +5,14 @@
 
 NS_STEPS = 4
 highest = lax.Precision.HIGHEST
+
+
+def group_lay(shard_in):
+    mesh_name = "rep"
+    axis_key = "grp"
+    for w in (axis_key, mesh_name):
+        shard_in = lax.psum(shard_in, w)
+    return shard_in
 
 
 def inverse_root(gram_matrix):
@@ -65,7 +73,7 @@
     ortho_gate = jnp.dot(left_gate, inverse_root(gram_gate), precision=highest)
     terms_query = right_terms(merged_query, ortho_query)
     terms_gate = right_terms(merged_gate, ortho_gate)
-    basis_new_query, basis_new_gate = lax.psum((terms_query, terms_gate), ("rep", "grp"))
+    basis_new_query, basis_new_gate = group_lay((terms_query, terms_gate))
     error_out_query, momentum_out_query, master_out_query = finish(
         merged_query, ortho_query, basis_new_query, momentum_query, master_query, replicas
     )

time: 370 us -> 493 us (1.33)
  waiting for transfers between devices: 200 us -> 265 us
  blocking collectives: 111 us -> 168 us
    psum x1 -> x2, waiting for transfers between devices: 74.1 us -> 144 us  [group_lay(): shard_in = lax.psum(shard_in, w)]
    psum x1 -> x2, blocking collectives: 22.7 us -> 57.5 us  [per_device(): lax.psum((jnp.dot(left_query.T, left_query, precision=highest), jnp.dot(l...]
    psum x1 -> x2, blocking collectives: 65.4 us -> 86.8 us  [the longest x1 62.6 us: per_device(): left_query, left_gate = lax.psum((local_query, local_gate), 'rep')]
    psum x1, waiting for transfers between devices: 83.3 us -> 76.3 us  [per_device(): left_query, left_gate = lax.psum((local_query, local_gate), 'rep')]
    unnamed x36 -> x33, local copies, waits for them, and re-layouts: 11.1 us -> 11.7 us
  transfers between devices with their start and end apart: 4 -> 5, of which waited for: 3 -> 4; matrix products, arithmetic and copies ran while one was open for 3% -> 2% of each run, Pallas kernels for 0% -> 0%
where the time goes in v1:
time: 493 us
  waiting for transfers between devices  265 us (54%)
  blocking collectives  168 us (34%)
  matrix products  28.4 us (6%)
  between operations  16.2 us (3%)
  local copies, waits for them, and re-layouts  11.7 us (2%)
    psum x2, waiting for transfers between devices, group_lay(): shard_in = lax.psum(shard_in, w)  144 us
    psum x1, waiting for transfers between devices, per_device(): left_query, left_gate = lax.psum((local_query, local_gate), 'rep')  76.3 us
    psum x1, blocking collectives, per_device(): left_query, left_gate = lax.psum((local_query, local_gate), 'rep')  62.6 us
    psum x2, blocking collectives, per_device(): lax.psum((jnp.dot(left_query.T, left_query, precision=highest), jnp.dot(l...  57.5 us
    all_gather x1, waiting for transfers between devices, per_device(): lax.all_gather(master_out_query.astype(jnp.bfloat16), 'grp', axis=0, tile...  45 us
    psum x1, blocking collectives, group_lay(): shard_in = lax.psum(shard_in, w)  24.2 us
    unnamed x1, blocking collectives  23.3 us
    unnamed x33, local copies, waits for them, and re-layouts  11.7 us
  transfers between devices with their start and end apart: 5, of which 4 were waited for; matrix products, arithmetic and copies ran while one was open for 2% of the time, Pallas kernels for 0%

profile of v1, /device:TPU:1, one launch (start us, length us, event | category | flops | bytes accessed | tf_op | source)
XLA Modules:
  0.0 492.5 jit_solution(8838899213449355816)
XLA Ops:
  7.2 1.5 fusion.15
  8.8 62.6 %psum.67 = f32[256,32]{0,1:T(8,128)S(1)} all-reduce(f32[256,32]{0,1:T(8,128)S(1)} %fusion.15), channel_id=1, replica_groups=mesh['rep'=16,'grp'=8] {'rep'}, use_global_device_ids=true, to_apply=%region_5.6 | all-reduce | flops 8192 | bytes 65536 | tf_op jit(solution)/shard_map/psum | solution.py:64
  71.6 34.8 %psum.68 = f32[32,32]{1,0:T(8,128)S(1)} all-reduce(f32[32,32]{1,0:T(8,128)S(1)} %fusion.35), channel_id=1, replica_groups=mesh['rep'=16,'grp'=8] {'grp'}, use_global_device_ids=true, to_apply=%region_6.7 | all-reduce | flops 1024 | bytes 8192 | tf_op jit(solution)/shard_map/psum | solution.py:65
  106.4 0.6 select_reduce_fusion
  107.0 0.8 fusion.8
  107.9 0.8 fusion.21
  110.6 0.2 fusion.40
  110.9 1.3 fusion.13
  112.2 24.2 %psum.69 = f32[256,32]{0,1:T(8,128)} all-reduce(f32[256,32]{0,1:T(8,128)S(1)} %fusion.13), channel_id=1, replica_groups=mesh['rep'=16,'grp'=8] {'grp'}, use_global_device_ids=true, to_apply=%region_8.9 | all-reduce | flops 8192 | bytes 65536 | tf_op jit(solution)/shard_map/psum | solution.py:14
  136.4 1.3 reduce
  137.7 4.1 fusion.2
  141.8 76.3 %all-reduce.10.cloned.1.call-done = (f32[256,32]{0,1:T(8,128)}, f32[256,32]{0,1:T(8,128)}, f32[1600]{0:T(1024)}) async-done(((f32[256,32]{0,1:T(8,128)}, f32[256,32]{0,1:T(8,128)}, f32[1600]{0:T(1024)}), (f32[256,32]{0,1:T(8,128)}, f32[256,32]{0,1:T(8,128)}, f32[1600]{0:T(1024)})) %all-reduce.10.cloned.1.call-update) | async-done | bytes 71952 | tf_op jit(solution)/shard_map/psum | solution.py:64
  218.1 1.0 fusion.29
  219.1 22.7 %psum.64 = f32[32,32]{1,0:T(8,128)S(1)} all-reduce(f32[32,32]{1,0:T(8,128)S(1)} %fusion.29), channel_id=1, replica_groups=mesh['rep'=16,'grp'=8] {'grp'}, use_global_device_ids=true, to_apply=%region_1.0 | all-reduce | flops 1024 | bytes 8192 | tf_op jit(solution)/shard_map/psum | solution.py:65
  241.8 0.6 select_reduce_fusion.1
  242.4 0.8 fusion.12
  243.3 0.8 fusion.20
  246.1 1.0 fusion.34
  247.1 3.8 fusion
  251.0 58.0 %all-reduce.6.cloned.1.call-done = f32[2048,32]{0,1:T(8,128)} async-done(((f32[2048,32]{0,1:T(8,128)}), f32[2048,32]{0,1:T(8,128)}) %all-reduce.6.cloned.1.call-update) | async-done | bytes 262160 | tf_op jit(solution)/shard_map/psum | solution.py:14
  309.1 1.4 fusion.27
  310.6 85.9 %all-reduce.8.cloned.1.call-done = f32[2048,32]{0,1:T(8,128)} async-done(((f32[2048,32]{0,1:T(8,128)}), f32[2048,32]{0,1:T(8,128)}) %all-reduce.8.cloned.1.call-update) | async-done | bytes 262160 | tf_op jit(solution)/shard_map/psum | solution.py:14
  396.5 8.2 %fusion.28 = (bf16[256,2048]{1,0:T(8,128)(2,1)}, f32[256,2048]{1,0:T(8,128)}, f32[256,2048]{1,0:T(8,128)}, f32[1,256,2048]{2,1,0:T(8,128)}) fusion(f32[256,2048]{1,0:T(8,128)} %param.17, f32[256,2048]{1,0:T(8,128)} %param.16, f32[1,256,2048]{2,1,0:T(8,128)S(1)} %copy-done.1, f32[1,256,2048]{2,1,0:T(8,128)} %param.14, f32[256,32]{0,1:T(8,128)S(1)} %fusion.34, ...), kind=kOutput, calls=%fused_computation.53 | convolution fusion | flops 205520896 | bytes 16023552 | tf_op jit(solution)/shard_map/dot_general | solution.py:35
  404.8 0.6 dynamic-slice
  406.1 0.6 fusion.26
  406.7 0.2 dynamic-update-slice
  406.9 23.3 %all-reduce = bf16[12800]{0:T(1024)(128)(2,1)} all-reduce(bf16[12800]{0:T(1024)(128)(2,1)S(1)} %dynamic-update-slice), channel_id=1, replica_groups=mesh['rep'=16,'grp'=8] {'grp'}, use_global_device_ids=true, to_apply=%add | all-reduce | flops 12800 | bytes 51200
  430.2 45.0 %all-gather.3.cloned.1.call-done = bf16[2048,2048]{1,0:T(8,128)(2,1)} async-done(((bf16[256,2048]{1,0:T(8,128)(2,1)}), bf16[2048,2048]{1,0:T(8,128)(2,1)}) %all-gather.3.cloned.1.call-update) | async-done | bytes 8388624 | tf_op jit(solution)/shard_map/all_gather | solution.py:87
  475.2 8.5 %copy.34 = bf16[2048,2048]{1,0:T(8,128)(2,1)} copy(bf16[2048,2048]{1,0:T(8,128)(2,1)} %all-gather.3.cloned.1.call-done) | data formatting | bytes 16777216
  483.7 0.7 copy.35
  484.4 1.0 copy.36
  485.4 0.6 copy.37
  (57 shorter events, 3.1 us)
Async XLA Ops:
  7.2 130.5 %copy-start = (f32[2048,32]{0,1:T(8,128)S(1)}, f32[2048,32]{0,1:T(8,128)}, u32[]{:S(2)}) copy-start(f32[2048,32]{0,1:T(8,128)} %param.15) | copy-start | bytes 786436
  7.2 130.5 %copy-start.1 = (f32[1,256,2048]{2,1,0:T(8,128)S(1)}, f32[1,256,2048]{2,1,0:T(8,128)}, u32[]{:S(2)}) copy-start(f32[1,256,2048]{2,1,0:T(8,128)} %param.13) | copy-start | bytes 6291460
  7.2 210.9 %all-reduce.10.cloned.1.call-start = ((), (), s32[]{:S(2)}) async-start(), calls=%async_computation.4 | async-start | bytes 147456 | tf_op jit(solution)/shard_map/psum | solution.py:64
  141.8 167.2 %all-reduce.6.cloned.1.call-start = ((), (), s32[]{:S(2)}) async-start(), calls=%async_computation | async-start | bytes 524288 | tf_op jit(solution)/shard_map/psum | solution.py:14
  247.0 62.0 %copy-start.2 = (f32[1,256,256]{2,1,0:T(8,128)S(1)}, f32[1,256,256]{2,1,0:T(8,128)}, u32[]{:S(2)}) copy-start(f32[1,256,256]{2,1,0:T(8,128)} %param.18) | copy-start | bytes 786436
  247.1 62.0 %copy-start.3 = (f32[1,256,256]{2,1,0:T(8,128)S(1)}, f32[1,256,256]{2,1,0:T(8,128)}, u32[]{:S(2)}) copy-start(f32[1,256,256]{2,1,0:T(8,128)} %param.19) | copy-start | bytes 786436
  247.1 62.0 %copy-start.6 = (f32[256,256]{1,0:T(8,128)S(1)}, f32[256,256]{1,0:T(8,128)}, u32[]{:S(2)}) copy-start(f32[256,256]{1,0:T(8,128)} %param.22) | copy-start | bytes 786436
  247.1 62.0 %copy-start.7 = (f32[256,256]{1,0:T(8,128)S(1)}, f32[256,256]{1,0:T(8,128)}, u32[]{:S(2)}) copy-start(f32[256,256]{1,0:T(8,128)} %param.21) | copy-start | bytes 786436
  247.1 62.0 %copy-start.8 = (f32[256,32]{0,1:T(8,128)S(1)}, f32[256,32]{0,1:T(8,128)}, u32[]{:S(2)}) copy-start(f32[256,32]{0,1:T(8,128)} %get-tuple-element.49) | copy-start | bytes 98308
  250.9 145.6 %all-reduce.8.cloned.1.call-start = ((), (), s32[]{:S(2)}) async-start(), calls=%async_computation.1 | async-start | bytes 524288 | tf_op jit(solution)/shard_map/psum | solution.py:14
  309.0 121.2 %all-gather.5.cloned.1.call-start = ((), (), s32[]{:S(2)}) async-start(), calls=%async_computation.3 | async-start | bytes 1179648 | tf_op jit(solution)/shard_map/all_gather | solution.py:88
  310.5 94.3 %copy-start.12 = (u32[128]{0:T(128)S(1)}, u32[128]{0:T(128)}, u32[]{:S(2)}) copy-start(u32[128]{0:T(128)} %constant.33) | copy-start | bytes 1540
  310.5 95.5 %copy-start.9 = (f32[1600]{0:T(1024)S(1)}, f32[1600]{0:T(1024)}, u32[]{:S(2)}) copy-start(f32[1600]{0:T(1024)} %param.25) | copy-start | bytes 19204
  310.5 95.5 %copy-start.10 = (f32[1600]{0:T(1024)S(1)}, f32[1600]{0:T(1024)}, u32[]{:S(2)}) copy-start(f32[1600]{0:T(1024)} %param.24) | copy-start | bytes 19204
  310.5 95.5 %copy-start.11 = (f32[1600]{0:T(1024)S(1)}, f32[1600]{0:T(1024)}, u32[]{:S(2)}) copy-start(f32[1600]{0:T(1024)} %get-tuple-element.15) | copy-start | bytes 19204
  310.5 164.6 %all-gather.3.cloned.1.call-start = ((), (), s32[]{:S(2)}) async-start(), calls=%async_computation.2 | async-start | bytes 9437184 | tf_op jit(solution)/shard_map/all_gather | solution.py:87
  475.2 8.6 %copy-start.4 = (f32[2048,32]{0,1:T(8,128)S(1)}, f32[2048,32]{0,1:T(8,128)}, u32[]{:S(2)}) copy-start(f32[2048,32]{0,1:T(8,128)} %all-reduce.8.cloned.1.call-done) | copy-start | bytes 786436
  475.2 9.3 %copy-start.5 = (bf16[2048,256]{1,0:T(8,128)(2,1)S(1)}, bf16[2048,256]{1,0:T(8,128)(2,1)}, u32[]{:S(2)}) copy-start(bf16[2048,256]{1,0:T(8,128)(2,1)} %all-gather.5.cloned.1.call-done) | copy-start | bytes 3145732
Sparse Core Ops, SparseCore 0:
  141.9 76.2 all-reduce.9
  251.0 57.9 all-reduce.5
  312.2 84.3 all-reduce.7
  398.8 24.3 all-gather.4
  425.4 49.7 all-gather.2
